TPU v7x, 128 devices: a whole 4x4x4 slice. The times are simulated.
128 devices in a mesh: section: 2 (over z_hi), seq: 8 (over x, z_lo), expert: 8 (over y, core).
Axes of the slice: x: 4, y: 4, z: 4 (z_hi: 2, z_lo: 2; z = z_hi * 2 + z_lo), core: 2. Of those that a mesh axis runs over, the one named last changes fastest.
Arguments:
- tokens: bfloat16 [2, 1024, 2048], P(None, ('seq', 'expert')), may hold values from -12 to 12
- prompt_lengths: int32 [2, 3], replicated, may hold values from 1 to 512, 1024 in all within a row
- cache_lengths: int32 [2, 3], replicated, may hold values from 1 to 1024, 2048 in all within a row
- kv_cache: bfloat16 [2, 2048, 2, 2048], P(None, 'seq', None, 'expert'), may hold values from -360 to 360
- attn_routes: int32 [2, 1024, 2], P(None, 'seq'), may hold values from 0 to 3, all different within a row
- ffn_routes: int32 [2, 1024, 2], P(None, ('seq', 'expert')), may hold values from 0 to 7, all different within a row; in each aligned block of 16 rows (0 to 15, 16 to 31, ..., all dimensions but the last counted through in order) at most 8 rows name the same one
- attn_gain: float32 [2048], replicated, may hold values from 0.1 to 1.9
- ffn_gain: float32 [2048], replicated, may hold values from 0.1 to 1.9
- attn_mix: bfloat16 [2048, 4], replicated, may hold values from -0.125 to 0.125
- query_weight: bfloat16 [2048, 4, 2048], P(None, None, 'expert'), may hold values from -0.125 to 0.125
- kv_weight: bfloat16 [2048, 2, 2048], P(None, None, 'expert'), may hold values from -0.125 to 0.125
- out_weight: bfloat16 [4, 2048, 2048], P(None, 'expert'), may hold values from -0.125 to 0.125
- ffn_mix: bfloat16 [2048, 8], replicated, may hold values from -0.125 to 0.125
- in_weight: bfloat16 [8, 2048, 2, 5632], P('expert', None, None, 'seq'), may hold values from -0.125 to 0.125
- down_weight: bfloat16 [8, 5632, 2048], P('expert', 'seq'), may hold values from -0.078125 to 0.078125
Outputs:
- layer_out: bfloat16 [2, 1024, 2048], P('section', ('seq', 'expert'))
Inputs may be any that keep to these rules, and one draw needn't show every extreme that they name: `prompt_lengths`: each row sums to 1024; its largest entry is 512. `cache_lengths`: each row sums to 2048; its largest entry is 1024. `attn_routes`: the two experts of a position differ; every expert is named somewhere. `ffn_routes`: the two experts of a position differ. Taking all micro-batches and positions in order, in each aligned block of 16 positions (the rows of one device) no expert is named more than 8 times, and some block names one exactly 8 times.
All inputs are finite; a program needn't handle non-finite values.
Results may differ from a plain program's by a relative error of at most 0.029.
Values may be sent and summed in bfloat16 or wider, within the bound.
A program may use at most 128 MiB of HBM per device.

v0:
```python
import jax
import jax.numpy as jnp
from jax import lax
from jax.sharding import PartitionSpec as P

HEAD_DIM = 128
EPS = 1e-06
THETA = 10000.0
NEGATIVE = -1e30


def passed_along(value, axis, steps):
    count = lax.axis_size(axis)
    initial, last = (max(0, -steps), min(count, count - steps))
    return lax.ppermute(value, axis, [(source, source + steps) for source in range(initial, last)])


def rms_scale(values, gain):
    widened = values.astype(jnp.float32)
    inverse = lax.rsqrt(jnp.mean(widened * widened, axis=-1, keepdims=True) + EPS)
    return (widened * inverse * gain).astype(jnp.bfloat16)


def segment_of(row_index, lengths):
    ends = jnp.cumsum(lengths)
    return jnp.sum((row_index[:, None] >= ends[None, :]).astype(jnp.int32), axis=1)


def positions(row_index, lengths, cached):
    ends = jnp.cumsum(lengths)
    segment = jnp.sum((row_index[:, None] >= ends[None, :]).astype(jnp.int32), axis=1)
    matched = segment[:, None] == jnp.arange(lengths.shape[0], dtype=jnp.int32)[None, :]
    begins = jnp.sum(jnp.where(matched, (ends - lengths)[None, :], 0), axis=1)
    offsets = jnp.sum(jnp.where(matched, cached[None, :], 0), axis=1)
    return (segment, offsets + row_index - begins)


def rotate(values, place):
    half_dim = values.shape[-1] // 2
    freq = THETA ** (-jnp.arange(half_dim, dtype=jnp.float32) / half_dim)
    angle = place.astype(jnp.float32)[:, None] * freq[None, :]
    shape = (values.shape[0],) + (1,) * (values.ndim - 2) + (half_dim,)
    cosine = jnp.cos(angle).reshape(shape)
    sine = jnp.sin(angle).reshape(shape)
    former = values[..., :half_dim]
    latter = values[..., half_dim:]
    return jnp.concatenate(
        [former * cosine - latter * sine, latter * cosine + former * sine], axis=-1
    )


def route_gates(normed, mixing, routes):
    logits = jnp.dot(normed, mixing, preferred_element_type=jnp.float32)
    chosen = jnp.take_along_axis(logits, routes, axis=1)
    leading = jax.nn.sigmoid(chosen[:, 0] - chosen[:, 1])
    return jnp.stack([leading, 1.0 - leading], axis=1)


def select_batch(values, batch):
    return lax.dynamic_index_in_dim(values, batch, 0, keepdims=False)


def attention_block(
    own_rows, lengths, cached, cache_rows, routes, gain, mixing, query_weight, kv_weight, out_weight
):
    gathered = lax.all_gather(own_rows, "expert", axis=0, tiled=True)
    count = gathered.shape[0]
    normed = rms_scale(gathered, gain)
    row_index = lax.axis_index("seq") * count + jnp.arange(count, dtype=jnp.int32)
    segment, place = positions(row_index, lengths, cached)
    gates = route_gates(normed, mixing, routes)
    experts = query_weight.shape[1]
    width = query_weight.shape[2]
    local_heads = width // HEAD_DIM
    query_all = jnp.dot(
        normed, query_weight.reshape(query_weight.shape[0], -1), preferred_element_type=jnp.float32
    )
    query_all = query_all.reshape(count, experts, local_heads, HEAD_DIM)
    query = jnp.take_along_axis(query_all, routes[:, :, None, None], axis=1)
    query = rotate(query, place).astype(jnp.bfloat16)
    queries = query.reshape(count * 2, local_heads, HEAD_DIM)
    projected = jnp.dot(
        normed, kv_weight.reshape(kv_weight.shape[0], -1), preferred_element_type=jnp.float32
    )
    projected = projected.reshape(count, 2, local_heads, HEAD_DIM)
    fresh_keys = rotate(projected[:, 0], place).astype(jnp.bfloat16).reshape(count, width)
    fresh_values = projected[:, 1].astype(jnp.bfloat16).reshape(count, width)
    fresh = jnp.stack([fresh_keys, fresh_values], axis=1)
    query_segment = jnp.repeat(segment, 2)
    query_index = jnp.repeat(row_index, 2)
    scale = HEAD_DIM ** (-0.5)
    slots = count * 2

    def absorb(carried, piece, allowed):
        row_top, row_total, row_sum = carried
        keys = piece[:, 0].reshape(-1, local_heads, HEAD_DIM)
        values = piece[:, 1].reshape(-1, local_heads, HEAD_DIM)
        scores = (
            jnp.einsum("qhd,khd->hqk", queries, keys, preferred_element_type=jnp.float32) * scale
        )
        scores = jnp.where(allowed[None], scores, NEGATIVE)
        new_top = jnp.maximum(row_top, jnp.max(scores, axis=2))
        weights = jnp.where(allowed[None], jnp.exp(scores - new_top[:, :, None]), 0.0)
        shrink = jnp.exp(row_top - new_top)
        row_total = row_total * shrink + jnp.sum(weights, axis=2)
        row_sum = row_sum * shrink[:, :, None] + jnp.einsum(
            "hqk,khd->hqd", weights.astype(jnp.bfloat16), values, preferred_element_type=jnp.float32
        )
        return (new_top, row_total, row_sum)

    initial = (
        jnp.full((local_heads, slots), NEGATIVE, jnp.float32),
        jnp.zeros((local_heads, slots), jnp.float32),
        jnp.zeros((local_heads, slots, HEAD_DIM), jnp.float32),
    )
    piece = lax.all_gather(cache_rows, "seq", axis=0, tiled=True)
    key_segment = segment_of(jnp.arange(piece.shape[0], dtype=jnp.int32), cached)
    allowed = query_segment[:, None] == key_segment[None, :]
    carried = absorb(initial, piece, allowed)
    piece = lax.all_gather(fresh, "seq", axis=0, tiled=True)
    key_index = jnp.arange(piece.shape[0], dtype=jnp.int32)
    key_segment = segment_of(key_index, lengths)
    allowed = (query_segment[:, None] == key_segment[None, :]) & (
        key_index[None, :] <= query_index[:, None]
    )
    row_top, row_total, row_sum = absorb(carried, piece, allowed)
    attended = (row_sum / row_total[:, :, None]).astype(jnp.bfloat16)
    attended = attended.transpose(1, 0, 2).reshape(count, 2, width)
    select = (routes[:, :, None] == jnp.arange(experts, dtype=jnp.int32)[None, None, :]).astype(
        jnp.float32
    )
    select = select * gates[:, :, None]
    spread = jnp.einsum("tka,tkd->tad", select, attended.astype(jnp.float32)).astype(jnp.bfloat16)
    spread = spread.reshape(count, experts * width)
    out_flat = out_weight.reshape(experts * width, -1)
    term = lax.psum_scatter(
        jnp.dot(spread, out_flat, preferred_element_type=jnp.float32).astype(jnp.bfloat16),
        "expert",
        scatter_dimension=0,
        tiled=True,
    ).astype(jnp.float32)
    return (own_rows.astype(jnp.float32) + term).astype(jnp.bfloat16)


def expert_hidden(rows, in_weight):
    single = in_weight[0]
    both = jnp.dot(rows, single.reshape(single.shape[0], -1), preferred_element_type=jnp.float32)
    both = both.reshape(rows.shape[0], 2, -1)
    return (jax.nn.silu(both[:, 0]) * both[:, 1]).astype(jnp.bfloat16)


def expert_block(middle, routes, gain, mixing, in_weight, down_weight):
    rows = middle.shape[0]
    features = middle.shape[1]
    normed = rms_scale(middle, gain)
    gates = route_gates(normed, mixing, routes)
    experts = mixing.shape[1]
    capacity = max(2, 4 * rows // experts)
    flat = routes.reshape(-1)
    member = (flat[:, None] == jnp.arange(experts, dtype=jnp.int32)[None, :]).astype(jnp.int32)
    earlier = jnp.cumsum(member, axis=0) - member
    slot = jnp.sum(earlier * member, axis=1)
    target = flat * capacity + slot
    table = (jnp.arange(experts * capacity, dtype=jnp.int32)[:, None] == target[None, :]).astype(
        jnp.bfloat16
    )
    table = jnp.sum(table.reshape(experts * capacity, rows, 2), axis=2)
    buffer = jnp.dot(table, normed, preferred_element_type=jnp.float32).astype(jnp.bfloat16)
    buffer = buffer.reshape(experts, capacity, features)
    seq_count = lax.axis_size("seq")
    copies = jnp.broadcast_to(buffer[None], (seq_count,) + buffer.shape)
    copies = copies.reshape(seq_count * experts, capacity, features)
    arrived = lax.all_to_all(copies, ("seq", "expert"), split_axis=0, concat_axis=0, tiled=True)
    flat_rows = arrived.reshape(-1, features)
    hidden = expert_hidden(flat_rows, in_weight)
    partial_value = jnp.dot(hidden, down_weight[0], preferred_element_type=jnp.float32)
    partial_value = partial_value.astype(jnp.bfloat16).reshape(arrived.shape)
    returned = lax.all_to_all(
        partial_value, ("seq", "expert"), split_axis=0, concat_axis=0, tiled=True
    )
    results = jnp.sum(
        returned.reshape(seq_count, experts, capacity, features).astype(jnp.float32), axis=0
    )
    picked = jnp.take(results.reshape(experts * capacity, features), target, axis=0).reshape(
        rows, 2, features
    )
    mixture = gates[:, 0:1] * picked[:, 0] + gates[:, 1:2] * picked[:, 1]
    return (middle.astype(jnp.float32) + mixture).astype(jnp.bfloat16)


def on_device(
    tokens,
    prompt_lengths,
    cache_lengths,
    kv_cache,
    attn_routes,
    ffn_routes,
    attn_gain,
    ffn_gain,
    attn_mix,
    query_weight,
    kv_weight,
    out_weight,
    ffn_mix,
    in_weight,
    down_weight,
):
    batches = tokens.shape[0]
    half_count = batches // 2
    section = lax.axis_index("section")

    def attend(batch):
        return attention_block(
            select_batch(tokens, batch),
            select_batch(prompt_lengths, batch),
            select_batch(cache_lengths, batch),
            select_batch(kv_cache, batch),
            select_batch(attn_routes, batch),
            attn_gain,
            attn_mix,
            query_weight,
            kv_weight,
            out_weight,
        )

    def finish(middle, batch):
        return expert_block(
            middle, select_batch(ffn_routes, batch), ffn_gain, ffn_mix, in_weight, down_weight
        )

    blank = jnp.zeros(tokens.shape[1:], jnp.bfloat16)
    first_section = section == 0

    def one_tick(incoming, tick):
        ahead = jnp.minimum(tick, batches - 1)
        behind = jnp.maximum(tick - 1, 0)
        attended_rows = attend(ahead)
        finished_rows = finish(incoming, behind)
        produced = jnp.where(first_section, attended_rows, finished_rows)
        passed = passed_along(produced, "section", 1)
        return (passed, produced)

    ticks = jnp.arange(batches + 1, dtype=jnp.int32)
    _, produced_all = lax.scan(one_tick, blank, ticks)
    finished = produced_all[1:]
    former_half = finished[:half_count]
    latter_half = finished[half_count:]
    returned = passed_along(former_half, "section", -1)
    return jnp.where(first_section, returned, latter_half)


def solution(mesh):
    return jax.shard_map(
        on_device,
        mesh=mesh,
        in_specs=(
            P(None, ("seq", "expert"), None),
            P(),
            P(),
            P(None, "seq", None, "expert"),
            P(None, "seq", None),
            P(None, ("seq", "expert"), None),
            P(),
            P(),
            P(),
            P(None, None, "expert"),
            P(None, None, "expert"),
            P(None, "expert", None),
            P(),
            P("expert", None, None, "seq"),
            P("expert", "seq", None),
        ),
        out_specs=P("section", ("seq", "expert"), None),
        check_vma=False,
    )
```

profile of v0, /device:TPU:0, one launch (start us, length us, event | category | flops | bytes accessed | tf_op | source)
XLA Modules:
  0.0 696.3 jit_solution(16072841294543308900)
XLA Ops:
  6.5 7.7 %copy.140 = bf16[2048,4,256]{0,2,1:T(8,128)(2,1)} copy(bf16[2048,4,256]{2,1,0:T(4,128)(2,1)} %param.26) | data formatting | bytes 8388608 | tf_op jit(solution)/shard_map/while | solution.py:244
  14.3 4.8 copy.142
  19.2 660.6 %while.14 = (s32[]{:T(128)}, bf16[16,2048]{1,0:T(8,128)(2,1)S(1)}, bf16[3,16,2048]{2,1,0:T(8,128)(2,1)}, pred[]{:T(512)}, s32[3]{0:T(128)S(1)}, /*index=5*/bf16[...) while((s32[]{:T(128)}, bf16[16,2048]{1,0:T(8,128)(2,1)S(1)}, ...), condition=%wide.region_19.20_spmd, body=%wide.region_0.19_spmd.sunk | while | flops 6617626624 | bytes 126714792 | solution.py:244
  20.5 13.7 %all-gather.5 = bf16[1,128,2048]{2,1,0:T(8,128)(2,1)S(1)} all-gather(bf16[1,16,2048]{2,1,0:T(8,128)(2,1)S(1)} %constant_dynamic-slice_fusion.10), channel_id=2, replica_groups=mesh['section'=2,'seq'=8,'expert'=8] {'expert'}, dimensions={1}, use_global_device_ids=true | all-gather | bytes 589824 | tf_op jit(solution)/shard_map/while/body/eval_jaxpr/all_gather | solution.py:66
  34.5 2.4 fusion.208
  41.6 8.9 %all-to-all-start = ((bf16[64,8,2048]{2,1,0:T(8,128)(2,1)}), bf16[64,8,2048]{2,1,0:T(8,128)(2,1)}, u32[]{:S(2)}, u32[]{:S(2)}) async-start(bf16[64,8,2048]{2,1,0:T(8,128)(2,1)} %bitcast.287), calls=%async_computation | async-start | bytes 4194304 | tf_op jit(solution)/shard_map/while/body/eval_jaxpr/all_to_all | solution.py:173
  54.5 3.8 fusion.202
  60.6 2.4 gather_fusion.3
  65.5 37.0 %all-gather.11.cloned.1.call-done = bf16[1024,2,256]{0,2,1:T(8,128)(2,1)} async-done(((bf16[128,2,256]{0,2,1:T(8,128)(2,1)}), bf16[1024,2,256]{0,2,1:T(8,128)(2,1)}) %all-gather.11.cloned.1.call-update) | async-done | bytes 1048592 | tf_op jit(solution)/shard_map/while/body/eval_jaxpr/all_gather | solution.py:120
  102.5 2.1 fusion.209
  106.5 6.0 fusion.195
  112.6 3.4 fusion.196
  116.0 10.0 %all-to-all-start.1 = ((bf16[64,8,2048]{2,1,0:T(8,128)(2,1)}), bf16[64,8,2048]{2,1,0:T(8,128)(2,1)S(1)}, u32[]{:S(2)}, u32[]{:S(2)}) async-start(bf16[64,8,2048]{2,1,0:T(8,128)(2,1)} %fusion.196), calls=%async_computation.1 | async-start | bytes 4194304 | tf_op jit(solution)/shard_map/while/body/eval_jaxpr/all_to_all | solution.py:178
  126.0 60.6 %all-gather.9.cloned.1.call-done = bf16[1,2048,2,256]{1,3,2,0:T(8,128)(2,1)} async-done(((bf16[1,256,2,256]{1,3,2,0:T(8,128)(2,1)}), bf16[1,2048,2,256]{1,3,2,0:T(8,128)(2,1)}) %all-gather.9.cloned.1.call-update) | async-done | bytes 2097168 | tf_op jit(solution)/shard_map/while/body/eval_jaxpr/all_gather | solution.py:116
  195.3 3.7 fusion.216
  200.4 32.2 %reduce-scatter.2.cloned.1.call-done = bf16[16,2048]{1,0:T(8,128)(2,1)} async-done(((bf16[128,2048]{1,0:T(8,128)(2,1)}), bf16[16,2048]{1,0:T(8,128)(2,1)}) %reduce-scatter.2.cloned.1.call-update) | async-done | bytes 65552 | tf_op jit(solution)/shard_map/while/body/eval_jaxpr/reduce_scatter | solution.py:136
  234.1 5.1 collective-permute-start
  242.4 13.1 %all-gather.5 = bf16[1,128,2048]{2,1,0:T(8,128)(2,1)S(1)} all-gather(bf16[1,16,2048]{2,1,0:T(8,128)(2,1)S(1)} %constant_dynamic-slice_fusion.10), channel_id=2, replica_groups=mesh['section'=2,'seq'=8,'expert'=8] {'expert'}, dimensions={1}, use_global_device_ids=true | all-gather | bytes 589824 | tf_op jit(solution)/shard_map/while/body/eval_jaxpr/all_gather | solution.py:66
  255.7 2.4 fusion.208
  262.9 6.4 all-to-all-start
  273.3 3.7 fusion.202
  279.4 2.4 gather_fusion.3
  284.3 38.8 %all-gather.11.cloned.1.call-done = bf16[1024,2,256]{0,2,1:T(8,128)(2,1)} async-done(((bf16[128,2,256]{0,2,1:T(8,128)(2,1)}), bf16[1024,2,256]{0,2,1:T(8,128)(2,1)}) %all-gather.11.cloned.1.call-update) | async-done | bytes 1048592 | tf_op jit(solution)/shard_map/while/body/eval_jaxpr/all_gather | solution.py:120
  323.1 2.1 fusion.209
  325.2 2.0 fusion.210
  327.2 6.0 fusion.195
  333.3 3.4 fusion.196
  336.6 10.1 %all-to-all-start.1 = ((bf16[64,8,2048]{2,1,0:T(8,128)(2,1)}), bf16[64,8,2048]{2,1,0:T(8,128)(2,1)S(1)}, u32[]{:S(2)}, u32[]{:S(2)}) async-start(bf16[64,8,2048]{2,1,0:T(8,128)(2,1)} %fusion.196), calls=%async_computation.1 | async-start | bytes 4194304 | tf_op jit(solution)/shard_map/while/body/eval_jaxpr/all_to_all | solution.py:178
  346.8 62.6 %all-gather.9.cloned.1.call-done = bf16[1,2048,2,256]{1,3,2,0:T(8,128)(2,1)} async-done(((bf16[1,256,2,256]{1,3,2,0:T(8,128)(2,1)}), bf16[1,2048,2,256]{1,3,2,0:T(8,128)(2,1)}) %all-gather.9.cloned.1.call-update) | async-done | bytes 2097168 | tf_op jit(solution)/shard_map/while/body/eval_jaxpr/all_gather | solution.py:116
  418.1 3.7 fusion.216
  423.3 27.6 %reduce-scatter.2.cloned.1.call-done = bf16[16,2048]{1,0:T(8,128)(2,1)} async-done(((bf16[128,2048]{1,0:T(8,128)(2,1)}), bf16[16,2048]{1,0:T(8,128)(2,1)}) %reduce-scatter.2.cloned.1.call-update) | async-done | bytes 65552 | tf_op jit(solution)/shard_map/while/body/eval_jaxpr/reduce_scatter | solution.py:136
  452.5 4.9 collective-permute-start
  460.6 13.1 %all-gather.5 = bf16[1,128,2048]{2,1,0:T(8,128)(2,1)S(1)} all-gather(bf16[1,16,2048]{2,1,0:T(8,128)(2,1)S(1)} %constant_dynamic-slice_fusion.10), channel_id=2, replica_groups=mesh['section'=2,'seq'=8,'expert'=8] {'expert'}, dimensions={1}, use_global_device_ids=true | all-gather | bytes 589824 | tf_op jit(solution)/shard_map/while/body/eval_jaxpr/all_gather | solution.py:66
  473.9 2.4 fusion.208
  481.1 6.6 all-to-all-start
  491.7 3.7 fusion.202
  497.7 2.4 gather_fusion.3
  502.6 39.1 %all-gather.11.cloned.1.call-done = bf16[1024,2,256]{0,2,1:T(8,128)(2,1)} async-done(((bf16[128,2,256]{0,2,1:T(8,128)(2,1)}), bf16[1024,2,256]{0,2,1:T(8,128)(2,1)}) %all-gather.11.cloned.1.call-update) | async-done | bytes 1048592 | tf_op jit(solution)/shard_map/while/body/eval_jaxpr/all_gather | solution.py:120
  541.8 2.1 fusion.209
  543.9 2.0 fusion.210
  545.9 6.0 fusion.195
  551.9 3.4 fusion.196
  555.3 9.8 %all-to-all-start.1 = ((bf16[64,8,2048]{2,1,0:T(8,128)(2,1)}), bf16[64,8,2048]{2,1,0:T(8,128)(2,1)S(1)}, u32[]{:S(2)}, u32[]{:S(2)}) async-start(bf16[64,8,2048]{2,1,0:T(8,128)(2,1)} %fusion.196), calls=%async_computation.1 | async-start | bytes 4194304 | tf_op jit(solution)/shard_map/while/body/eval_jaxpr/all_to_all | solution.py:178
  565.2 64.6 %all-gather.9.cloned.1.call-done = bf16[1,2048,2,256]{1,3,2,0:T(8,128)(2,1)} async-done(((bf16[1,256,2,256]{1,3,2,0:T(8,128)(2,1)}), bf16[1,2048,2,256]{1,3,2,0:T(8,128)(2,1)}) %all-gather.9.cloned.1.call-update) | async-done | bytes 2097168 | tf_op jit(solution)/shard_map/while/body/eval_jaxpr/all_gather | solution.py:116
  638.5 3.7 fusion.216
  643.6 27.7 %reduce-scatter.2.cloned.1.call-done = bf16[16,2048]{1,0:T(8,128)(2,1)} async-done(((bf16[128,2048]{1,0:T(8,128)(2,1)}), bf16[16,2048]{1,0:T(8,128)(2,1)}) %reduce-scatter.2.cloned.1.call-update) | async-done | bytes 65552 | tf_op jit(solution)/shard_map/while/body/eval_jaxpr/reduce_scatter | solution.py:136
  672.9 5.0 collective-permute-start
  681.9 6.4 collective-permute-done.1
  (339 shorter events, 87.0 us)
Async XLA Ops:
  6.5 7.7 %copy-start.3 = (bf16[2048,2,256]{2,1,0:T(2,128)(2,1)S(1)}, bf16[2048,2,256]{2,1,0:T(2,128)(2,1)}, u32[]{:S(2)}) copy-start(bf16[2048,2,256]{2,1,0:T(2,128)(2,1)} %param.27) | copy-start | bytes 6291460
  14.2 4.9 copy-start.2
  14.2 4.9 copy-start.4
  14.2 4.9 copy-start.5
  14.3 4.9 copy-start.6
  14.3 4.9 copy-start.7
  14.3 4.9 copy-start.8
  14.3 4.9 copy-start.9
  14.3 4.9 copy-start.11
  14.3 4.9 copy-start.12
  19.2 83.3 %all-gather.11.cloned.1.call-start = ((), (), s32[]{:S(2)}) async-start(), calls=%async_computation.4 | async-start | bytes 1179648 | tf_op jit(solution)/shard_map/while/body/eval_jaxpr/all_gather | solution.py:120
  41.6 64.9 %all-to-all-start = ((bf16[64,8,2048]{2,1,0:T(8,128)(2,1)}), bf16[64,8,2048]{2,1,0:T(8,128)(2,1)}, u32[]{:S(2)}, u32[]{:S(2)}) async-start(bf16[64,8,2048]{2,1,0:T(8,128)(2,1)} %bitcast.287), calls=%async_computation | async-start | bytes 4194304 | tf_op jit(solution)/shard_map/while/body/eval_jaxpr/all_to_all | solution.py:173
  50.5 136.1 %all-gather.9.cloned.1.call-start = ((), (), s32[]{:S(2)}) async-start(), calls=%async_computation.3 | async-start | bytes 2359296 | tf_op jit(solution)/shard_map/while/body/eval_jaxpr/all_gather | solution.py:116
  106.5 6.0 copy-start.10
  116.0 83.1 %all-to-all-start.1 = ((bf16[64,8,2048]{2,1,0:T(8,128)(2,1)}), bf16[64,8,2048]{2,1,0:T(8,128)(2,1)S(1)}, u32[]{:S(2)}, u32[]{:S(2)}) async-start(bf16[64,8,2048]{2,1,0:T(8,128)(2,1)} %fusion.196), calls=%async_computation.1 | async-start | bytes 4194304 | tf_op jit(solution)/shard_map/while/body/eval_jaxpr/all_to_all | solution.py:178
  125.9 106.7 %reduce-scatter.2.cloned.1.call-start = ((), (), s32[]{:S(2)}) async-start(), calls=%async_computation.5 | async-start | bytes 589824 | tf_op jit(solution)/shard_map/while/body/eval_jaxpr/reduce_scatter | solution.py:136
  188.3 1.6 copy-start
  192.1 1.4 copy-start.1
  234.1 6.9 collective-permute-start
  241.1 82.0 %all-gather.11.cloned.1.call-start = ((), (), s32[]{:S(2)}) async-start(), calls=%async_computation.4 | async-start | bytes 1179648 | tf_op jit(solution)/shard_map/while/body/eval_jaxpr/all_gather | solution.py:120
  262.9 64.3 %all-to-all-start = ((bf16[64,8,2048]{2,1,0:T(8,128)(2,1)}), bf16[64,8,2048]{2,1,0:T(8,128)(2,1)}, u32[]{:S(2)}, u32[]{:S(2)}) async-start(bf16[64,8,2048]{2,1,0:T(8,128)(2,1)} %bitcast.287), calls=%async_computation | async-start | bytes 4194304 | tf_op jit(solution)/shard_map/while/body/eval_jaxpr/all_to_all | solution.py:173
  269.3 140.1 %all-gather.9.cloned.1.call-start = ((), (), s32[]{:S(2)}) async-start(), calls=%async_computation.3 | async-start | bytes 2359296 | tf_op jit(solution)/shard_map/while/body/eval_jaxpr/all_gather | solution.py:116
  327.2 6.1 copy-start.10
  336.6 85.3 %all-to-all-start.1 = ((bf16[64,8,2048]{2,1,0:T(8,128)(2,1)}), bf16[64,8,2048]{2,1,0:T(8,128)(2,1)S(1)}, u32[]{:S(2)}, u32[]{:S(2)}) async-start(bf16[64,8,2048]{2,1,0:T(8,128)(2,1)} %fusion.196), calls=%async_computation.1 | async-start | bytes 4194304 | tf_op jit(solution)/shard_map/while/body/eval_jaxpr/all_to_all | solution.py:178
  346.7 104.2 %reduce-scatter.2.cloned.1.call-start = ((), (), s32[]{:S(2)}) async-start(), calls=%async_computation.5 | async-start | bytes 589824 | tf_op jit(solution)/shard_map/while/body/eval_jaxpr/reduce_scatter | solution.py:136
  411.1 1.6 copy-start
  415.0 1.4 copy-start.1
  452.5 6.8 collective-permute-start
  459.3 82.5 %all-gather.11.cloned.1.call-start = ((), (), s32[]{:S(2)}) async-start(), calls=%async_computation.4 | async-start | bytes 1179648 | tf_op jit(solution)/shard_map/while/body/eval_jaxpr/all_gather | solution.py:120
  481.1 64.8 %all-to-all-start = ((bf16[64,8,2048]{2,1,0:T(8,128)(2,1)}), bf16[64,8,2048]{2,1,0:T(8,128)(2,1)}, u32[]{:S(2)}, u32[]{:S(2)}) async-start(bf16[64,8,2048]{2,1,0:T(8,128)(2,1)} %bitcast.287), calls=%async_computation | async-start | bytes 4194304 | tf_op jit(solution)/shard_map/while/body/eval_jaxpr/all_to_all | solution.py:173
  487.7 142.1 %all-gather.9.cloned.1.call-start = ((), (), s32[]{:S(2)}) async-start(), calls=%async_computation.3 | async-start | bytes 2359296 | tf_op jit(solution)/shard_map/while/body/eval_jaxpr/all_gather | solution.py:116
  545.9 6.0 copy-start.10
  555.3 87.0 %all-to-all-start.1 = ((bf16[64,8,2048]{2,1,0:T(8,128)(2,1)}), bf16[64,8,2048]{2,1,0:T(8,128)(2,1)S(1)}, u32[]{:S(2)}, u32[]{:S(2)}) async-start(bf16[64,8,2048]{2,1,0:T(8,128)(2,1)} %fusion.196), calls=%async_computation.1 | async-start | bytes 4194304 | tf_op jit(solution)/shard_map/while/body/eval_jaxpr/all_to_all | solution.py:178
  565.1 106.2 %reduce-scatter.2.cloned.1.call-start = ((), (), s32[]{:S(2)}) async-start(), calls=%async_computation.5 | async-start | bytes 589824 | tf_op jit(solution)/shard_map/while/body/eval_jaxpr/reduce_scatter | solution.py:136
  631.5 1.6 copy-start
  635.3 1.4 copy-start.1
  672.9 6.9 collective-permute-start
  680.6 7.7 %collective-permute-start.1 = (bf16[1,16,2048]{2,1,0:T(8,128)(2,1)S(1)}, bf16[1,16,2048]{2,1,0:T(8,128)(2,1)S(1)}, u32[]{:S(2)}, u32[]{:S(2)}) collective-permute-start(bf16[1,16,2048]{2,1,0:T(8,128)(2,1)S(1)} %slice.118), channel_id=1, source_target_pairs={{64,0},{65,1},{66,2},{67,3},{68,4},{69,5},{70,6},{71,7},{72,8},{73... | collective-permute-start | bytes 196616 | tf_op jit(solution)/shard_map/ppermute | solution.py:15
Sparse Core Ops, SparseCore 0:
  38.3 64.0 all-gather.10
  104.0 82.4 all-gather.8
  199.1 33.4 reduce-scatter.1
  259.6 63.4 all-gather.10
  324.5 84.8 all-gather.8
  422.0 28.8 reduce-scatter.1
  477.8 63.9 all-gather.10
  543.3 86.3 all-gather.8
  642.3 28.9 reduce-scatter.1
where the time goes:
time: 698 us; the launch traced here: 696 us
  waiting for transfers between devices  402 us (58%)
  matrix products  78.5 us (11%)
  starting transfers between devices  68.3 us (10%)
  local copies, waits for them, and re-layouts  62.6 us (9%)
  blocking collectives  39.9 us (6%)
  other arithmetic  26 us (4%)
  between operations  13.2 us (2%)
    all_gather x3, waiting for transfers between devices, attention_block(): piece = lax.all_gather(cache_rows, 'seq', axis=0, tiled=True)  188 us
    all_gather x3, waiting for transfers between devices, attention_block(): piece = lax.all_gather(fresh, 'seq', axis=0, tiled=True)  115 us
    reduce_scatter x3, waiting for transfers between devices, attention_block(): lax.psum_scatter(jnp.dot(spread, out_flat, preferred_element_type=jnp.flo...  87.5 us
    all_gather x3, blocking collectives, attention_block(): gathered = lax.all_gather(own_rows, 'expert', axis=0, tiled=True)  39.9 us
    all_to_all x3, starting transfers between devices, expert_block(): lax.all_to_all(partial_value, ('seq', 'expert'), split_axis=0, concat_axi...  29.9 us
    all_to_all x3, starting transfers between devices, expert_block(): lax.all_to_all(copies, ('seq', 'expert'), split_axis=0, concat_axis=0, ti...  21.9 us
    dot_general x3, matrix products, expert_hidden(): jnp.dot(rows, single.reshape(single.shape[0], -1), preferred_element_type...  18.1 us
    ppermute x4, starting transfers between devices, passed_along(): lax.ppermute(value, axis, [(source, source + steps) for source in range(i...  16.2 us
  transfers between devices with their start and end apart: 19, of which 13 were waited for; matrix products, arithmetic and copies ran while one was open for 19% of the time, Pallas kernels for 0%

commit v1 on v0

--- a/solution.py
+++ b/solution.py
@@ -7,6 +7,12 @@
 EPS = 1e-06
 THETA = 10000.0
 NEGATIVE = -1e30
+
+
+def replace_sizes_over_axis(unit, ndim_at):
+    parts_out = jnp.stack([unit for _ in range(lax.axis_size("seq"))])
+    mid_arr = lax.all_to_all(parts_out, "seq", 0, 0)
+    return jnp.concatenate(mid_arr, ndim_at)
 
 
 def passed_along(value, axis, steps):
@@ -117,7 +123,7 @@
     key_segment = segment_of(jnp.arange(piece.shape[0], dtype=jnp.int32), cached)
     allowed = query_segment[:, None] == key_segment[None, :]
     carried = absorb(initial, piece, allowed)
-    piece = lax.all_gather(fresh, "seq", axis=0, tiled=True)
+    piece = replace_sizes_over_axis(fresh, 0)
     key_index = jnp.arange(piece.shape[0], dtype=jnp.int32)
     key_segment = segment_of(key_index, lengths)
     allowed = (query_segment[:, None] == key_segment[None, :]) & (

time: 698 us -> 510 us (0.73)
  waiting for transfers between devices: 402 us -> 198 us
  starting transfers between devices: 68.3 us -> 84.8 us
    all_gather x3, waiting for transfers between devices: 188 us -> 0.06 us  [attention_block(): piece = lax.all_gather(cache_rows, 'seq', axis=0, tiled=True)]
    all_gather x3 -> x0, waiting for transfers between devices: 115 us -> none  [attention_block(): piece = lax.all_gather(fresh, 'seq', axis=0, tiled=True)]
    all_to_all x3, waiting for transfers between devices: 0.01 us -> 67.5 us  [expert_block(): lax.all_to_all(copies, ('seq', 'expert'), split_axis=0, concat_axis=0, ti...]
    all_to_all x3, waiting for transfers between devices: 0.01 us -> 48.3 us  [expert_block(): lax.all_to_all(partial_value, ('seq', 'expert'), split_axis=0, concat_axi...]
    reduce_scatter x3, waiting for transfers between devices: 87.5 us -> 43.7 us  [attention_block(): lax.psum_scatter(jnp.dot(spread, out_flat, preferred_element_type=jnp.flo...]
    all_to_all x0 -> x3, waiting for transfers between devices: none -> 26 us  [replace_sizes_over_axis(): mid_arr = lax.all_to_all(parts_out, 'seq', 0, 0)]
    all_to_all x0 -> x3, starting transfers between devices: none -> 15.2 us  [replace_sizes_over_axis(): mid_arr = lax.all_to_all(parts_out, 'seq', 0, 0)]
  transfers between devices with their start and end apart: 19 -> 19, of which waited for: 13 -> 16; matrix products, arithmetic and copies ran while one was open for 19% -> 27% of each run, Pallas kernels for 0% -> 0%
where the time goes in v1:
time: 510 us; the launch traced here: 507 us
  waiting for transfers between devices  198 us (39%)
  starting transfers between devices  84.8 us (17%)
  matrix products  78.2 us (15%)
  local copies, waits for them, and re-layouts  63.5 us (12%)
  blocking collectives  39.9 us (8%)
  other arithmetic  24.1 us (5%)
  between operations  13.5 us (3%)
  loops' own time  5.28 us (1%)
    all_to_all x3, waiting for transfers between devices, expert_block(): lax.all_to_all(copies, ('seq', 'expert'), split_axis=0, concat_axis=0, ti...  67.5 us
    all_to_all x3, waiting for transfers between devices, expert_block(): lax.all_to_all(partial_value, ('seq', 'expert'), split_axis=0, concat_axi...  48.3 us
    reduce_scatter x3, waiting for transfers between devices, attention_block(): lax.psum_scatter(jnp.dot(spread, out_flat, preferred_element_type=jnp.flo...  43.7 us
    all_gather x3, blocking collectives, attention_block(): gathered = lax.all_gather(own_rows, 'expert', axis=0, tiled=True)  39.9 us
    all_to_all x3, starting transfers between devices, expert_block(): lax.all_to_all(partial_value, ('seq', 'expert'), split_axis=0, concat_axi...  29.7 us
    all_to_all x3, waiting for transfers between devices, replace_sizes_over_axis(): mid_arr = lax.all_to_all(parts_out, 'seq', 0, 0)  26 us
    all_to_all x3, starting transfers between devices, expert_block(): lax.all_to_all(copies, ('seq', 'expert'), split_axis=0, concat_axis=0, ti...  23 us
    dot_general x3, matrix products, expert_hidden(): jnp.dot(rows, single.reshape(single.shape[0], -1), preferred_element_type...  18.1 us
  transfers between devices with their start and end apart: 19, of which 16 were waited for; matrix products, arithmetic and copies ran while one was open for 27% of the time, Pallas kernels for 0%

profile of v1, /device:TPU:0, one launch (start us, length us, event | category | flops | bytes accessed | tf_op | source)
XLA Modules:
  0.0 507.0 jit_solution(8303923412617056251)
XLA Ops:
  6.5 7.7 %copy.145 = bf16[2048,4,256]{0,2,1:T(8,128)(2,1)} copy(bf16[2048,4,256]{2,1,0:T(4,128)(2,1)} %param.26) | data formatting | bytes 8388608 | tf_op jit(solution)/shard_map/while | solution.py:250
  14.3 4.8 copy.147
  19.2 471.0 %while.14 = (s32[]{:T(128)}, bf16[16,2048]{1,0:T(8,128)(2,1)S(1)}, bf16[3,16,2048]{2,1,0:T(8,128)(2,1)}, pred[]{:T(512)}, s32[3]{0:T(128)S(1)}, /*index=5*/bf16[...) while((s32[]{:T(128)}, bf16[16,2048]{1,0:T(8,128)(2,1)S(1)}, ...), condition=%wide.region_19.20_spmd, body=%wide.region_0.19_spmd.sunk | while | flops 6617626624 | bytes 129598360 | solution.py:250
  22.6 13.7 %all-gather.5 = bf16[1,128,2048]{2,1,0:T(8,128)(2,1)S(1)} all-gather(bf16[1,16,2048]{2,1,0:T(8,128)(2,1)S(1)} %constant_dynamic-slice_fusion.10), channel_id=2, replica_groups=mesh['section'=2,'seq'=8,'expert'=8] {'expert'}, dimensions={1}, use_global_device_ids=true | all-gather | bytes 589824 | tf_op jit(solution)/shard_map/while/body/eval_jaxpr/all_gather | solution.py:72
  36.5 2.4 fusion.211
  40.9 5.7 %all-to-all-start.2 = ((bf16[8,128,2,256]{1,3,2,0:T(8,128)(2,1)}), bf16[8,128,2,256]{1,3,2,0:T(8,128)(2,1)S(1)}, u32[]{:S(2)}, u32[]{:S(2)}) async-start(bf16[8,128,2,256]{1,3,2,0:T(8,128)(2,1)} %stack.13), calls=%async_computation.2 | async-start | bytes 2097152 | tf_op jit(solution)/shard_map/while/body/eval_jaxpr/all_to_all | solution.py:14
  50.1 2.4 gather_fusion.3
  52.9 3.7 fusion.205
  57.0 8.2 %all-to-all-done.2 = bf16[8,128,2,256]{1,3,2,0:T(8,128)(2,1)S(1)} async-done(((bf16[8,128,2,256]{1,3,2,0:T(8,128)(2,1)}), bf16[8,128,2,256]{1,3,2,0:T(8,128)(2,1)S(1)}, u32[]{:S(2)}, u32[]{:S(2)}) %all-to-all-start.2) | async-done | bytes 1048608 | tf_op jit(solution)/shard_map/while/body/eval_jaxpr/all_to_all | solution.py:14
  66.8 8.9 %all-to-all-start = ((bf16[64,8,2048]{2,1,0:T(8,128)(2,1)}), bf16[64,8,2048]{2,1,0:T(8,128)(2,1)}, u32[]{:S(2)}, u32[]{:S(2)}) async-start(bf16[64,8,2048]{2,1,0:T(8,128)(2,1)} %bitcast.296), calls=%async_computation | async-start | bytes 4194304 | tf_op jit(solution)/shard_map/while/body/eval_jaxpr/all_to_all | solution.py:179
  82.9 23.3 %all-to-all-done = bf16[64,8,2048]{2,1,0:T(8,128)(2,1)} async-done(((bf16[64,8,2048]{2,1,0:T(8,128)(2,1)}), bf16[64,8,2048]{2,1,0:T(8,128)(2,1)}, u32[]{:S(2)}, u32[]{:S(2)}) %all-to-all-start) | async-done | bytes 2097184 | tf_op jit(solution)/shard_map/while/body/eval_jaxpr/all_to_all | solution.py:179
  106.2 6.0 %fusion.198 = f32[512,2,704]{0,2,1:T(8,128)S(1)} fusion(bf16[1,2048,2,704]{1,3,2,0:T(8,128)(2,1)} %get-tuple-element.722, bf16[64,8,2048]{2,1,0:T(8,128)(2,1)} %all-to-all-done), kind=kOutput, calls=%fused_computation.4.clone.1 | convolution fusion | flops 2952790016 | bytes 10747904 | tf_op jit(solution)/shard_map/while/body/eval_jaxpr/dot_general | solution.py:153
  112.3 3.4 fusion.199
  115.6 6.1 %all-to-all-start.1 = ((bf16[64,8,2048]{2,1,0:T(8,128)(2,1)}), bf16[64,8,2048]{2,1,0:T(8,128)(2,1)S(1)}, u32[]{:S(2)}, u32[]{:S(2)}) async-start(bf16[64,8,2048]{2,1,0:T(8,128)(2,1)} %fusion.199), calls=%async_computation.1 | async-start | bytes 4194304 | tf_op jit(solution)/shard_map/while/body/eval_jaxpr/all_to_all | solution.py:184
  130.5 3.7 fusion.219
  134.3 16.1 %all-to-all-done.1 = bf16[64,8,2048]{2,1,0:T(8,128)(2,1)S(1)} async-done(((bf16[64,8,2048]{2,1,0:T(8,128)(2,1)}), bf16[64,8,2048]{2,1,0:T(8,128)(2,1)S(1)}, u32[]{:S(2)}, u32[]{:S(2)}) %all-to-all-start.1) | async-done | bytes 2097184 | tf_op jit(solution)/shard_map/while/body/eval_jaxpr/all_to_all | solution.py:184
  151.7 16.7 %reduce-scatter.2.cloned.1.call-done = bf16[16,2048]{1,0:T(8,128)(2,1)} async-done(((bf16[128,2048]{1,0:T(8,128)(2,1)}), bf16[16,2048]{1,0:T(8,128)(2,1)}) %reduce-scatter.2.cloned.1.call-update) | async-done | bytes 65552 | tf_op jit(solution)/shard_map/while/body/eval_jaxpr/reduce_scatter | solution.py:142
  170.0 5.2 %collective-permute-start = (bf16[16,2048]{1,0:T(8,128)(2,1)S(1)}, bf16[16,2048]{1,0:T(8,128)(2,1)S(1)}, u32[]{:S(2)}, u32[]{:S(2)}) collective-permute-start(bf16[16,2048]{1,0:T(8,128)(2,1)S(1)} %get-tuple-element.644), channel_id=1, source_target_pairs={{0,64},{1,65},{2,66},{3,67},{4,68},{5,69},{6,70},{7,71},{8,72},{9,... | collective-permute-start | bytes 196616 | tf_op jit(solution)/shard_map/while/body/eval_jaxpr/ppermute | solution.py:21
  180.4 13.1 %all-gather.5 = bf16[1,128,2048]{2,1,0:T(8,128)(2,1)S(1)} all-gather(bf16[1,16,2048]{2,1,0:T(8,128)(2,1)S(1)} %constant_dynamic-slice_fusion.10), channel_id=2, replica_groups=mesh['section'=2,'seq'=8,'expert'=8] {'expert'}, dimensions={1}, use_global_device_ids=true | all-gather | bytes 589824 | tf_op jit(solution)/shard_map/while/body/eval_jaxpr/all_gather | solution.py:72
  193.7 2.4 fusion.211
  198.1 4.8 all-to-all-start.2
  206.4 2.4 gather_fusion.3
  209.2 3.7 fusion.205
  213.3 8.9 %all-to-all-done.2 = bf16[8,128,2,256]{1,3,2,0:T(8,128)(2,1)S(1)} async-done(((bf16[8,128,2,256]{1,3,2,0:T(8,128)(2,1)}), bf16[8,128,2,256]{1,3,2,0:T(8,128)(2,1)S(1)}, u32[]{:S(2)}, u32[]{:S(2)}) %all-to-all-start.2) | async-done | bytes 1048608 | tf_op jit(solution)/shard_map/while/body/eval_jaxpr/all_to_all | solution.py:14
  223.8 7.1 %all-to-all-start = ((bf16[64,8,2048]{2,1,0:T(8,128)(2,1)}), bf16[64,8,2048]{2,1,0:T(8,128)(2,1)}, u32[]{:S(2)}, u32[]{:S(2)}) async-start(bf16[64,8,2048]{2,1,0:T(8,128)(2,1)} %bitcast.296), calls=%async_computation | async-start | bytes 4194304 | tf_op jit(solution)/shard_map/while/body/eval_jaxpr/all_to_all | solution.py:179
  238.1 22.1 %all-to-all-done = bf16[64,8,2048]{2,1,0:T(8,128)(2,1)} async-done(((bf16[64,8,2048]{2,1,0:T(8,128)(2,1)}), bf16[64,8,2048]{2,1,0:T(8,128)(2,1)}, u32[]{:S(2)}, u32[]{:S(2)}) %all-to-all-start) | async-done | bytes 2097184 | tf_op jit(solution)/shard_map/while/body/eval_jaxpr/all_to_all | solution.py:179
  260.2 6.0 %fusion.198 = f32[512,2,704]{0,2,1:T(8,128)S(1)} fusion(bf16[1,2048,2,704]{1,3,2,0:T(8,128)(2,1)} %get-tuple-element.722, bf16[64,8,2048]{2,1,0:T(8,128)(2,1)} %all-to-all-done), kind=kOutput, calls=%fused_computation.4.clone.1 | convolution fusion | flops 2952790016 | bytes 10747904 | tf_op jit(solution)/shard_map/while/body/eval_jaxpr/dot_general | solution.py:153
  266.2 3.4 fusion.199
  269.6 11.8 %all-to-all-start.1 = ((bf16[64,8,2048]{2,1,0:T(8,128)(2,1)}), bf16[64,8,2048]{2,1,0:T(8,128)(2,1)S(1)}, u32[]{:S(2)}, u32[]{:S(2)}) async-start(bf16[64,8,2048]{2,1,0:T(8,128)(2,1)} %fusion.199), calls=%async_computation.1 | async-start | bytes 4194304 | tf_op jit(solution)/shard_map/while/body/eval_jaxpr/all_to_all | solution.py:184
  290.3 3.7 fusion.219
  294.0 16.1 %all-to-all-done.1 = bf16[64,8,2048]{2,1,0:T(8,128)(2,1)S(1)} async-done(((bf16[64,8,2048]{2,1,0:T(8,128)(2,1)}), bf16[64,8,2048]{2,1,0:T(8,128)(2,1)S(1)}, u32[]{:S(2)}, u32[]{:S(2)}) %all-to-all-start.1) | async-done | bytes 2097184 | tf_op jit(solution)/shard_map/while/body/eval_jaxpr/all_to_all | solution.py:184
  311.5 13.5 %reduce-scatter.2.cloned.1.call-done = bf16[16,2048]{1,0:T(8,128)(2,1)} async-done(((bf16[128,2048]{1,0:T(8,128)(2,1)}), bf16[16,2048]{1,0:T(8,128)(2,1)}) %reduce-scatter.2.cloned.1.call-update) | async-done | bytes 65552 | tf_op jit(solution)/shard_map/while/body/eval_jaxpr/reduce_scatter | solution.py:142
  326.6 5.1 %collective-permute-start = (bf16[16,2048]{1,0:T(8,128)(2,1)S(1)}, bf16[16,2048]{1,0:T(8,128)(2,1)S(1)}, u32[]{:S(2)}, u32[]{:S(2)}) collective-permute-start(bf16[16,2048]{1,0:T(8,128)(2,1)S(1)} %get-tuple-element.644), channel_id=1, source_target_pairs={{0,64},{1,65},{2,66},{3,67},{4,68},{5,69},{6,70},{7,71},{8,72},{9,... | collective-permute-start | bytes 196616 | tf_op jit(solution)/shard_map/while/body/eval_jaxpr/ppermute | solution.py:21
  337.0 13.1 %all-gather.5 = bf16[1,128,2048]{2,1,0:T(8,128)(2,1)S(1)} all-gather(bf16[1,16,2048]{2,1,0:T(8,128)(2,1)S(1)} %constant_dynamic-slice_fusion.10), channel_id=2, replica_groups=mesh['section'=2,'seq'=8,'expert'=8] {'expert'}, dimensions={1}, use_global_device_ids=true | all-gather | bytes 589824 | tf_op jit(solution)/shard_map/while/body/eval_jaxpr/all_gather | solution.py:72
  354.6 4.8 all-to-all-start.2
  363.0 2.4 gather_fusion.3
  365.7 3.7 fusion.205
  369.8 8.9 %all-to-all-done.2 = bf16[8,128,2,256]{1,3,2,0:T(8,128)(2,1)S(1)} async-done(((bf16[8,128,2,256]{1,3,2,0:T(8,128)(2,1)}), bf16[8,128,2,256]{1,3,2,0:T(8,128)(2,1)S(1)}, u32[]{:S(2)}, u32[]{:S(2)}) %all-to-all-start.2) | async-done | bytes 1048608 | tf_op jit(solution)/shard_map/while/body/eval_jaxpr/all_to_all | solution.py:14
  380.3 7.1 %all-to-all-start = ((bf16[64,8,2048]{2,1,0:T(8,128)(2,1)}), bf16[64,8,2048]{2,1,0:T(8,128)(2,1)}, u32[]{:S(2)}, u32[]{:S(2)}) async-start(bf16[64,8,2048]{2,1,0:T(8,128)(2,1)} %bitcast.296), calls=%async_computation | async-start | bytes 4194304 | tf_op jit(solution)/shard_map/while/body/eval_jaxpr/all_to_all | solution.py:179
  394.7 22.1 %all-to-all-done = bf16[64,8,2048]{2,1,0:T(8,128)(2,1)} async-done(((bf16[64,8,2048]{2,1,0:T(8,128)(2,1)}), bf16[64,8,2048]{2,1,0:T(8,128)(2,1)}, u32[]{:S(2)}, u32[]{:S(2)}) %all-to-all-start) | async-done | bytes 2097184 | tf_op jit(solution)/shard_map/while/body/eval_jaxpr/all_to_all | solution.py:179
  416.8 6.0 %fusion.198 = f32[512,2,704]{0,2,1:T(8,128)S(1)} fusion(bf16[1,2048,2,704]{1,3,2,0:T(8,128)(2,1)} %get-tuple-element.722, bf16[64,8,2048]{2,1,0:T(8,128)(2,1)} %all-to-all-done), kind=kOutput, calls=%fused_computation.4.clone.1 | convolution fusion | flops 2952790016 | bytes 10747904 | tf_op jit(solution)/shard_map/while/body/eval_jaxpr/dot_general | solution.py:153
  422.8 3.4 fusion.199
  426.2 11.8 %all-to-all-start.1 = ((bf16[64,8,2048]{2,1,0:T(8,128)(2,1)}), bf16[64,8,2048]{2,1,0:T(8,128)(2,1)S(1)}, u32[]{:S(2)}, u32[]{:S(2)}) async-start(bf16[64,8,2048]{2,1,0:T(8,128)(2,1)} %fusion.199), calls=%async_computation.1 | async-start | bytes 4194304 | tf_op jit(solution)/shard_map/while/body/eval_jaxpr/all_to_all | solution.py:184
  446.8 3.7 fusion.219
  450.6 16.1 %all-to-all-done.1 = bf16[64,8,2048]{2,1,0:T(8,128)(2,1)S(1)} async-done(((bf16[64,8,2048]{2,1,0:T(8,128)(2,1)}), bf16[64,8,2048]{2,1,0:T(8,128)(2,1)S(1)}, u32[]{:S(2)}, u32[]{:S(2)}) %all-to-all-start.1) | async-done | bytes 2097184 | tf_op jit(solution)/shard_map/while/body/eval_jaxpr/all_to_all | solution.py:184
  468.0 13.5 %reduce-scatter.2.cloned.1.call-done = bf16[16,2048]{1,0:T(8,128)(2,1)} async-done(((bf16[128,2048]{1,0:T(8,128)(2,1)}), bf16[16,2048]{1,0:T(8,128)(2,1)}) %reduce-scatter.2.cloned.1.call-update) | async-done | bytes 65552 | tf_op jit(solution)/shard_map/while/body/eval_jaxpr/reduce_scatter | solution.py:142
  483.1 5.2 %collective-permute-start = (bf16[16,2048]{1,0:T(8,128)(2,1)S(1)}, bf16[16,2048]{1,0:T(8,128)(2,1)S(1)}, u32[]{:S(2)}, u32[]{:S(2)}) collective-permute-start(bf16[16,2048]{1,0:T(8,128)(2,1)S(1)} %get-tuple-element.644), channel_id=1, source_target_pairs={{0,64},{1,65},{2,66},{3,67},{4,68},{5,69},{6,70},{7,71},{8,72},{9,... | collective-permute-start | bytes 196616 | tf_op jit(solution)/shard_map/while/body/eval_jaxpr/ppermute | solution.py:21
  492.3 6.4 %collective-permute-done.1 = bf16[1,16,2048]{2,1,0:T(8,128)(2,1)S(1)} collective-permute-done((bf16[1,16,2048]{2,1,0:T(8,128)(2,1)S(1)}, bf16[1,16,2048]{2,1,0:T(8,128)(2,1)S(1)}, u32[]{:S(2)}, u32[]{:S(2)}) %collective-permute-start.1) | collective-permute-done | bytes 65568 | tf_op jit(solution)/shard_map/ppermute | solution.py:21
  (342 shorter events, 98.2 us)
Async XLA Ops:
  6.5 7.7 %copy-start.3 = (bf16[2048,2,256]{2,1,0:T(2,128)(2,1)S(1)}, bf16[2048,2,256]{2,1,0:T(2,128)(2,1)}, u32[]{:S(2)}) copy-start(bf16[2048,2,256]{2,1,0:T(2,128)(2,1)} %param.27) | copy-start | bytes 6291460
  14.2 4.9 copy-start.2
  14.2 4.9 copy-start.4
  14.2 4.9 copy-start.5
  14.3 4.9 copy-start.6
  14.3 4.9 copy-start.7
  14.3 4.9 copy-start.8
  14.3 4.9 copy-start.9
  14.3 4.9 copy-start.11
  14.3 4.9 copy-start.12
  19.2 102.6 %all-gather.8.cloned.1.call-start = ((), (), s32[]{:S(2)}) async-start(), calls=%async_computation.4 | async-start | bytes 2359296 | tf_op jit(solution)/shard_map/while/body/eval_jaxpr/all_gather | solution.py:122
  40.9 24.2 %all-to-all-start.2 = ((bf16[8,128,2,256]{1,3,2,0:T(8,128)(2,1)}), bf16[8,128,2,256]{1,3,2,0:T(8,128)(2,1)S(1)}, u32[]{:S(2)}, u32[]{:S(2)}) async-start(bf16[8,128,2,256]{1,3,2,0:T(8,128)(2,1)} %stack.13), calls=%async_computation.2 | async-start | bytes 2097152 | tf_op jit(solution)/shard_map/while/body/eval_jaxpr/all_to_all | solution.py:14
  66.8 39.4 %all-to-all-start = ((bf16[64,8,2048]{2,1,0:T(8,128)(2,1)}), bf16[64,8,2048]{2,1,0:T(8,128)(2,1)}, u32[]{:S(2)}, u32[]{:S(2)}) async-start(bf16[64,8,2048]{2,1,0:T(8,128)(2,1)} %bitcast.296), calls=%async_computation | async-start | bytes 4194304 | tf_op jit(solution)/shard_map/while/body/eval_jaxpr/all_to_all | solution.py:179
  106.2 6.0 %copy-start.10 = (bf16[1,704,2048]{2,1,0:T(8,128)(2,1)S(1)}, bf16[1,704,2048]{2,1,0:T(8,128)(2,1)}, u32[]{:S(2)}) copy-start(bf16[1,704,2048]{2,1,0:T(8,128)(2,1)} %get-tuple-element.723) | copy-start | bytes 8650756 | tf_op jit(solution)/shard_map/while
  115.6 34.8 %all-to-all-start.1 = ((bf16[64,8,2048]{2,1,0:T(8,128)(2,1)}), bf16[64,8,2048]{2,1,0:T(8,128)(2,1)S(1)}, u32[]{:S(2)}, u32[]{:S(2)}) async-start(bf16[64,8,2048]{2,1,0:T(8,128)(2,1)} %fusion.199), calls=%async_computation.1 | async-start | bytes 4194304 | tf_op jit(solution)/shard_map/while/body/eval_jaxpr/all_to_all | solution.py:184
  121.7 46.7 %reduce-scatter.2.cloned.1.call-start = ((), (), s32[]{:S(2)}) async-start(), calls=%async_computation.5 | async-start | bytes 589824 | tf_op jit(solution)/shard_map/while/body/eval_jaxpr/reduce_scatter | solution.py:142
  123.5 1.6 copy-start
  127.3 1.4 copy-start.1
  170.0 7.1 %collective-permute-start = (bf16[16,2048]{1,0:T(8,128)(2,1)S(1)}, bf16[16,2048]{1,0:T(8,128)(2,1)S(1)}, u32[]{:S(2)}, u32[]{:S(2)}) collective-permute-start(bf16[16,2048]{1,0:T(8,128)(2,1)S(1)} %get-tuple-element.644), channel_id=1, source_target_pairs={{0,64},{1,65},{2,66},{3,67},{4,68},{5,69},{6,70},{7,71},{8,72},{9,... | collective-permute-start | bytes 196616 | tf_op jit(solution)/shard_map/while/body/eval_jaxpr/ppermute | solution.py:21
  177.1 104.5 %all-gather.8.cloned.1.call-start = ((), (), s32[]{:S(2)}) async-start(), calls=%async_computation.4 | async-start | bytes 2359296 | tf_op jit(solution)/shard_map/while/body/eval_jaxpr/all_gather | solution.py:122
  198.1 24.1 %all-to-all-start.2 = ((bf16[8,128,2,256]{1,3,2,0:T(8,128)(2,1)}), bf16[8,128,2,256]{1,3,2,0:T(8,128)(2,1)S(1)}, u32[]{:S(2)}, u32[]{:S(2)}) async-start(bf16[8,128,2,256]{1,3,2,0:T(8,128)(2,1)} %stack.13), calls=%async_computation.2 | async-start | bytes 2097152 | tf_op jit(solution)/shard_map/while/body/eval_jaxpr/all_to_all | solution.py:14
  223.8 36.4 %all-to-all-start = ((bf16[64,8,2048]{2,1,0:T(8,128)(2,1)}), bf16[64,8,2048]{2,1,0:T(8,128)(2,1)}, u32[]{:S(2)}, u32[]{:S(2)}) async-start(bf16[64,8,2048]{2,1,0:T(8,128)(2,1)} %bitcast.296), calls=%async_computation | async-start | bytes 4194304 | tf_op jit(solution)/shard_map/while/body/eval_jaxpr/all_to_all | solution.py:179
  260.2 6.0 %copy-start.10 = (bf16[1,704,2048]{2,1,0:T(8,128)(2,1)S(1)}, bf16[1,704,2048]{2,1,0:T(8,128)(2,1)}, u32[]{:S(2)}) copy-start(bf16[1,704,2048]{2,1,0:T(8,128)(2,1)} %get-tuple-element.723) | copy-start | bytes 8650756 | tf_op jit(solution)/shard_map/while
  269.6 40.5 %all-to-all-start.1 = ((bf16[64,8,2048]{2,1,0:T(8,128)(2,1)}), bf16[64,8,2048]{2,1,0:T(8,128)(2,1)S(1)}, u32[]{:S(2)}, u32[]{:S(2)}) async-start(bf16[64,8,2048]{2,1,0:T(8,128)(2,1)} %fusion.199), calls=%async_computation.1 | async-start | bytes 4194304 | tf_op jit(solution)/shard_map/while/body/eval_jaxpr/all_to_all | solution.py:184
  281.5 43.5 %reduce-scatter.2.cloned.1.call-start = ((), (), s32[]{:S(2)}) async-start(), calls=%async_computation.5 | async-start | bytes 589824 | tf_op jit(solution)/shard_map/while/body/eval_jaxpr/reduce_scatter | solution.py:142
  283.3 1.6 copy-start
  287.1 1.4 copy-start.1
  326.6 7.0 %collective-permute-start = (bf16[16,2048]{1,0:T(8,128)(2,1)S(1)}, bf16[16,2048]{1,0:T(8,128)(2,1)S(1)}, u32[]{:S(2)}, u32[]{:S(2)}) collective-permute-start(bf16[16,2048]{1,0:T(8,128)(2,1)S(1)} %get-tuple-element.644), channel_id=1, source_target_pairs={{0,64},{1,65},{2,66},{3,67},{4,68},{5,69},{6,70},{7,71},{8,72},{9,... | collective-permute-start | bytes 196616 | tf_op jit(solution)/shard_map/while/body/eval_jaxpr/ppermute | solution.py:21
  333.6 104.5 %all-gather.8.cloned.1.call-start = ((), (), s32[]{:S(2)}) async-start(), calls=%async_computation.4 | async-start | bytes 2359296 | tf_op jit(solution)/shard_map/while/body/eval_jaxpr/all_gather | solution.py:122
  354.6 24.1 %all-to-all-start.2 = ((bf16[8,128,2,256]{1,3,2,0:T(8,128)(2,1)}), bf16[8,128,2,256]{1,3,2,0:T(8,128)(2,1)S(1)}, u32[]{:S(2)}, u32[]{:S(2)}) async-start(bf16[8,128,2,256]{1,3,2,0:T(8,128)(2,1)} %stack.13), calls=%async_computation.2 | async-start | bytes 2097152 | tf_op jit(solution)/shard_map/while/body/eval_jaxpr/all_to_all | solution.py:14
  380.3 36.4 %all-to-all-start = ((bf16[64,8,2048]{2,1,0:T(8,128)(2,1)}), bf16[64,8,2048]{2,1,0:T(8,128)(2,1)}, u32[]{:S(2)}, u32[]{:S(2)}) async-start(bf16[64,8,2048]{2,1,0:T(8,128)(2,1)} %bitcast.296), calls=%async_computation | async-start | bytes 4194304 | tf_op jit(solution)/shard_map/while/body/eval_jaxpr/all_to_all | solution.py:179
  416.8 6.0 %copy-start.10 = (bf16[1,704,2048]{2,1,0:T(8,128)(2,1)S(1)}, bf16[1,704,2048]{2,1,0:T(8,128)(2,1)}, u32[]{:S(2)}) copy-start(bf16[1,704,2048]{2,1,0:T(8,128)(2,1)} %get-tuple-element.723) | copy-start | bytes 8650756 | tf_op jit(solution)/shard_map/while
  426.2 40.5 %all-to-all-start.1 = ((bf16[64,8,2048]{2,1,0:T(8,128)(2,1)}), bf16[64,8,2048]{2,1,0:T(8,128)(2,1)S(1)}, u32[]{:S(2)}, u32[]{:S(2)}) async-start(bf16[64,8,2048]{2,1,0:T(8,128)(2,1)} %fusion.199), calls=%async_computation.1 | async-start | bytes 4194304 | tf_op jit(solution)/shard_map/while/body/eval_jaxpr/all_to_all | solution.py:184
  438.0 43.5 %reduce-scatter.2.cloned.1.call-start = ((), (), s32[]{:S(2)}) async-start(), calls=%async_computation.5 | async-start | bytes 589824 | tf_op jit(solution)/shard_map/while/body/eval_jaxpr/reduce_scatter | solution.py:142
  439.8 1.6 copy-start
  443.6 1.4 copy-start.1
  483.1 7.1 %collective-permute-start = (bf16[16,2048]{1,0:T(8,128)(2,1)S(1)}, bf16[16,2048]{1,0:T(8,128)(2,1)S(1)}, u32[]{:S(2)}, u32[]{:S(2)}) collective-permute-start(bf16[16,2048]{1,0:T(8,128)(2,1)S(1)} %get-tuple-element.644), channel_id=1, source_target_pairs={{0,64},{1,65},{2,66},{3,67},{4,68},{5,69},{6,70},{7,71},{8,72},{9,... | collective-permute-start | bytes 196616 | tf_op jit(solution)/shard_map/while/body/eval_jaxpr/ppermute | solution.py:21
  491.1 7.7 %collective-permute-start.1 = (bf16[1,16,2048]{2,1,0:T(8,128)(2,1)S(1)}, bf16[1,16,2048]{2,1,0:T(8,128)(2,1)S(1)}, u32[]{:S(2)}, u32[]{:S(2)}) collective-permute-start(bf16[1,16,2048]{2,1,0:T(8,128)(2,1)S(1)} %slice.118), channel_id=1, source_target_pairs={{64,0},{65,1},{66,2},{67,3},{68,4},{69,5},{70,6},{71,7},{72,8},{73... | collective-permute-start | bytes 196616 | tf_op jit(solution)/shard_map/ppermute | solution.py:21
Sparse Core Ops, SparseCore 0:
  22.7 94.1 all-gather.7
  134.4 34.0 reduce-scatter.1
  180.5 90.2 all-gather.7
  294.1 30.8 reduce-scatter.1
  337.0 90.3 all-gather.7
  450.6 30.8 reduce-scatter.1
